TPU v7x, 128 devices: a whole 4x4x4 slice. The times are simulated.
128 devices in a mesh: row: 16 (over z_hi, y, core), col: 8 (over z_lo, x).
Axes of the slice: x: 4, y: 4, z: 4 (z_hi: 2, z_lo: 2; z = z_hi * 2 + z_lo), core: 2. Of those that a mesh axis runs over, the one named last changes fastest.
Arguments:
- multispectral: bfloat16 [2, 32768, 4096], P(None, 'row', 'col'), may hold values from -6 to 6
- hyperspectral: bfloat16 [96, 8192, 1024], P(None, 'row', 'col'), may hold values from -6 to 6
- row_start: float32 [32768, 128], P(('row', 'col')), may hold values from -6 to 6
- col_factor: bfloat16 [4096, 128], P('col', 'row'), may hold values from -0.09375 to 0.09375
- band_factor: float32 [96, 128], replicated, may hold values from -2 to 2
- response: float32 [2, 96], replicated, may hold values from 0.2 to 1
- blur_taps: float32 [9], replicated, may hold values from 0.2 to 1
- offsets: int32 [9], replicated, may hold values from -8 to 8, as said below
Outputs:
- row_factor: float32 [32768, 128], P(('row', 'col'))
- residual: float32 [32768, 128], P(('row', 'col'))
Inputs may be any that keep to these rules, and one draw needn't show every extreme that they name: 9 distinct offsets; -8 and 8 are always among them.
All inputs are finite; a program needn't handle non-finite values.
Results may differ from a plain program's by a relative error of at most 0.0023.
Values may be sent and summed in bfloat16 or wider, within the bound.
A program may use at most 128 MiB of HBM per device.

v0:
```python
import jax
import jax.numpy as jnp
from jax import lax
from jax.sharding import PartitionSpec as P

DEC = 4
W = 8
ITERS = 4
RIDGE_TERM = 0.1
FULL_PRECISION = lax.Precision.HIGHEST


def extended(cells, sides, width):
    for axis, dim in sides:
        count = lax.axis_size(axis)
        head = lax.slice_in_dim(cells, 0, width, axis=dim)
        tail = lax.slice_in_dim(cells, cells.shape[dim] - width, cells.shape[dim], axis=dim)
        cells = jnp.concatenate(
            [
                lax.ppermute(tail, axis, [(i, (i + 1) % count) for i in range(count)]),
                cells,
                lax.ppermute(head, axis, [((i + 1) % count, i) for i in range(count)]),
            ],
            axis=dim,
        )
    return cells


def down_matrix(weights, offsets, rows_out, rows_in):
    outer = lax.broadcasted_iota(jnp.int32, (rows_out, rows_in), 0)
    inner = lax.broadcasted_iota(jnp.int32, (rows_out, rows_in), 1)
    total = jnp.zeros((rows_out, rows_in), jnp.float32)
    for number in range(weights.shape[0]):
        target = DEC * outer + offsets[number] + W
        total = total + jnp.where(inner == target, weights[number], jnp.float32(0.0))
    return total


def up_matrix(weights, offsets, rows_in, low_margin):
    rows_out = (rows_in - 2 * low_margin) * DEC
    outer = lax.broadcasted_iota(jnp.int32, (rows_out, rows_in), 0)
    inner = lax.broadcasted_iota(jnp.int32, (rows_out, rows_in), 1)
    total = jnp.zeros((rows_out, rows_in), jnp.float32)
    for number in range(weights.shape[0]):
        target = outer + DEC * low_margin - offsets[number]
        total = total + jnp.where(DEC * inner == target, weights[number], jnp.float32(0.0))
    return total


def apply_band(matrix, values):
    return jnp.dot(matrix, values.astype(jnp.float32), precision=FULL_PRECISION)


def body(
    multispectral, hyperspectral, row_start, col_factor, band_factor, response, blur_taps, offsets
):
    low_reach = (W + DEC - 1) // DEC
    columns = lax.all_gather(col_factor, "row", axis=1, tiled=True)
    column_wide = extended(columns, (("col", 0),), W)
    column_down = down_matrix(blur_taps, offsets, columns.shape[0] // DEC, column_wide.shape[0])
    coarse_columns = apply_band(column_down, column_wide)
    merged = jnp.dot(response, band_factor, precision=FULL_PRECISION)
    multi_pairs = (merged[:, None, :] * columns.astype(jnp.float32)[None, :, :]).astype(
        jnp.bfloat16
    )
    hyper_pairs = (band_factor[:, None, :] * coarse_columns[None, :, :]).astype(jnp.bfloat16)
    multi_part = jnp.einsum(
        "kij,kjr->ir", multispectral, multi_pairs, preferred_element_type=jnp.float32
    )
    hyper_part = jnp.einsum(
        "kij,kjr->ir", hyperspectral, hyper_pairs, preferred_element_type=jnp.float32
    )
    column_part = jnp.einsum("jr,js->rs", columns, columns, preferred_element_type=jnp.float32)
    coarse_part = jnp.einsum("jr,js->rs", coarse_columns, coarse_columns, precision=FULL_PRECISION)
    column_gram, coarse_gram = lax.psum((column_part, coarse_part), "col")
    band_gram = jnp.dot(band_factor.T, band_factor, precision=FULL_PRECISION)
    merged_gram = jnp.dot(merged.T, merged, precision=FULL_PRECISION)
    hyper_gram = coarse_gram * band_gram
    multi_gram = column_gram * merged_gram
    multi_sums, hyper_sums = lax.psum((multi_part, hyper_part), "col")
    start_rows = lax.all_gather(row_start, "col", axis=0, tiled=True)

    def fine_rim(values, breadth):
        return extended(values, (("row", 0),), breadth)

    def coarse_rim(values):
        return extended(values, (("row", 0),), low_reach)

    def inner_sum(first_field, second_field):
        return lax.psum(jnp.sum(first_field * second_field), "row")

    fine_rows = start_rows.shape[0]
    coarse_rows = fine_rows // DEC
    lifting = up_matrix(blur_taps, offsets, coarse_rows + 2 * low_reach, low_reach)
    lowering = down_matrix(blur_taps, offsets, coarse_rows, fine_rows + 2 * W)

    def operate(values):
        fine_wide = fine_rim(values, W)
        coarse_wide = coarse_rim(apply_band(lowering, fine_wide))
        restored = apply_band(lifting, coarse_wide)
        return (
            jnp.dot(restored, hyper_gram, precision=FULL_PRECISION)
            + jnp.dot(values, multi_gram, precision=FULL_PRECISION)
            + RIDGE_TERM * values
        )

    right_side = apply_band(lifting, coarse_rim(hyper_sums)) + multi_sums
    solution = start_rows
    residual = right_side - operate(solution)
    direction = residual
    norm_now = inner_sum(residual, residual)
    for iteration in range(ITERS):
        mapped = operate(direction)
        step_size = norm_now / inner_sum(direction, mapped)
        solution = solution + step_size * direction
        residual = residual - step_size * mapped
        norm_next = inner_sum(residual, residual)
        direction = residual + norm_next / norm_now * direction
        norm_now = norm_next
    portion = solution.shape[0] // lax.axis_size("col")
    corner = lax.axis_index("col") * portion
    solution = lax.dynamic_slice_in_dim(solution, corner, portion, 0)
    residual = lax.dynamic_slice_in_dim(residual, corner, portion, 0)
    return (solution, residual)


def solution(mesh):
    in_specs = (
        P(None, "row", "col"),
        P(None, "row", "col"),
        P(("row", "col"), None),
        P("col", "row"),
        P(),
        P(),
        P(),
        P(),
    )
    out_specs = (P(("row", "col"), None), P(("row", "col"), None))
    return jax.shard_map(body, mesh=mesh, in_specs=in_specs, out_specs=out_specs, check_vma=False)
```

profile of v0, /device:TPU:0, one launch (start us, length us, event | category | flops | bytes accessed | tf_op | source)
XLA Modules:
  0.0 721.7 jit_solution(4614198952941534308)
XLA Ops:
  7.2 25.9 %all_gather.7 = bf16[512,128]{0,1:T(8,128)(2,1)S(1)} all-gather(bf16[512,8]{0,1:T(8,128)(2,1)} %param.11), channel_id=1, replica_groups=mesh['row'=16,'col'=8] {'row'}, dimensions={1}, use_global_device_ids=true | all-gather | bytes 139264 | tf_op jit(solution)/shard_map/all_gather | solution.py:58
  52.6 6.3 fusion.50
  59.9 8.2 %fusion.14 = f32[512,128]{0,1:T(8,128)} fusion(bf16[96,512,128]{2,1,0:T(8,128)(2,1)} %param.9, f32[128,128]{0,1:T(8,128)S(1)} %copy.10, f32[96,128]{1,0:T(8,128)S(1)} %copy-done.4), kind=kOutput, calls=%fused_computation.33 | convolution fusion | flops 1613758464 | bytes 12959744 | tf_op jit(solution)/shard_map/kij,kjr->ir/dot_general | solution.py:70
  79.9 62.0 %all-reduce.4.cloned.1.call-done = (f32[128,128]{1,0:T(8,128)}, f32[128,128]{1,0:T(8,128)}, f32[2048,128]{1,0:T(8,128)}, f32[512,128]{0,1:T(8,128)}) async-done(((f32[128,128]{1,0:T(8,128)}, f32[128,128]{1,0:T(8,128)}, f32[2048,128]{1,0:T(8,128)}, f32[512,128]{0,1:T(8,128)}), (f32[128,128]{1,0:T(8,128)}, f32[128,128]{1,0:T(8,128)}, f32[2048,128]{1,0:T(8,128)}, ...) | async-done | bytes 1441808 | tf_op jit(solution)/shard_map/psum | solution.py:75
  143.0 39.1 %all-gather.2.cloned.1.call-done = f32[2048,128]{1,0:T(8,128)} async-done(((f32[256,128]{1,0:T(8,128)}), f32[2048,128]{1,0:T(8,128)}) %all-gather.2.cloned.1.call-update) | async-done | bytes 1048592 | tf_op jit(solution)/shard_map/all_gather | solution.py:81
  182.8 5.5 collective-permute-start.5
  189.7 15.4 %fusion.13 = f32[512,128]{1,0:T(8,128)S(1)} fusion(f32[]{:T(128)} %bitcast.17, s32[512]{0:T(512)S(1)} %get-tuple-element.63, f32[]{:T(128)} %bitcast.15, s32[512]{0:T(512)S(1)} %get-tuple-element.64, f32[]{:T(128)} %bitcast.13, s32[512]{0:T(512)S(1)} %get-tuple-element.65, f32[]{:T(128)} %bitcast.11, s32[512]{0:T(512)S(1)} %get-tuple-element.66, ...), kind=kOutput, calls=%fused_computation.32 | convolution fusion | flops 1651200000 | bytes 1337380 | tf_op jit(solution)/shard_map/dot_general | solution.py:51
  205.1 5.4 collective-permute-start.7
  210.9 5.7 collective-permute-start.3
  216.6 14.6 %fusion.19 = f32[2048,128]{1,0:T(8,128)S(1)} fusion(f32[]{:T(128)} %bitcast.17, f32[]{:T(128)} %bitcast.15, f32[]{:T(128)} %bitcast.13, f32[]{:T(128)} %bitcast.11, f32[]{:T(128)} %bitcast.9, f32[]{:T(128)} %bitcast.7, f32[]{:T(128)} %bitcast.5, f32[]{:T(128)} %bitcast.3, f32[]{:T(128)} %bitcast.1, s32[516]{0:T(1024)S(1)} %iota_multiply_fusion, ...), kind=kOutput, calls=%fused_computation.40 | convolution fusion | flops 1650803712 | bytes 1388596 | tf_op jit(solution)/shard_map/dot_general | solution.py:51
  233.4 15.0 %fusion.3 = f32[2048,128]{1,0:T(8,128)S(1)} fusion(f32[2048,128]{1,0:T(8,128)S(1)} %fusion.5, f32[2048,128]{1,0:T(8,128)S(1)} %copy-done.8, f32[]{:T(128)} %bitcast.17, f32[]{:T(128)} %bitcast.15, f32[]{:T(128)} %bitcast.13, f32[]{:T(128)} %bitcast.11, f32[]{:T(128)} %bitcast.9, f32[]{:T(128)} %bitcast.7, f32[]{:T(128)} %bitcast.5, f32[]{:T(128)} %bitcast.3, ...), kind=kOutput, calls=%fused_computation.18 | convolution fusion | flops 1651328000 | bytes 3485748 | tf_op jit(solution)/shard_map/dot_general | solution.py:51
  248.4 5.5 collective-permute-start.9
  255.3 14.2 %fusion.12 = f32[512,128]{1,0:T(8,128)S(1)} fusion(f32[]{:T(128)} %bitcast.17, s32[512]{0:T(512)S(1)} %get-tuple-element.63, f32[]{:T(128)} %bitcast.15, s32[512]{0:T(512)S(1)} %get-tuple-element.64, f32[]{:T(128)} %bitcast.13, s32[512]{0:T(512)S(1)} %get-tuple-element.65, f32[]{:T(128)} %bitcast.11, s32[512]{0:T(512)S(1)} %get-tuple-element.66, ...), kind=kOutput, calls=%fused_computation.31 | convolution fusion | flops 1651200000 | bytes 1337380 | tf_op jit(solution)/shard_map/dot_general | solution.py:51
  269.6 5.8 collective-permute-start.11
  276.7 14.7 %fusion.18 = f32[2048,128]{1,0:T(8,128)S(1)} fusion(f32[]{:T(128)} %bitcast.17, f32[]{:T(128)} %bitcast.15, f32[]{:T(128)} %bitcast.13, f32[]{:T(128)} %bitcast.11, f32[]{:T(128)} %bitcast.9, f32[]{:T(128)} %bitcast.7, f32[]{:T(128)} %bitcast.5, f32[]{:T(128)} %bitcast.3, f32[]{:T(128)} %bitcast.1, s32[516]{0:T(1024)S(1)} %iota_multiply_fusion, ...), kind=kOutput, calls=%fused_computation.39 | convolution fusion | flops 1650803712 | bytes 1388596 | tf_op jit(solution)/shard_map/dot_general | solution.py:51
  294.1 39.1 %all-reduce = (f32[]{:T(128)}, f32[]{:T(128)}) all-reduce(f32[]{:T(128)} %get-tuple-element.3, f32[]{:T(128)} %get-tuple-element.2), channel_id=1, replica_groups=mesh['row'=16,'col'=8] {'row'}, use_global_device_ids=true, to_apply=%region_5.6 | all-reduce | flops 2 | bytes 16 | tf_op jit(solution)/shard_map/psum | solution.py:90
  335.4 33.9 %psum.90 = f32[]{:T(128)} all-reduce(f32[]{:T(128)} %multiply_reduce_fusion.5), channel_id=1, replica_groups=mesh['row'=16,'col'=8] {'row'}, use_global_device_ids=true, to_apply=%region_9.10 | all-reduce | flops 1 | bytes 8 | tf_op jit(solution)/shard_map/psum | solution.py:90
  371.0 5.3 collective-permute-start.13
  377.7 14.1 %fusion.11 = f32[512,128]{1,0:T(8,128)S(1)} fusion(f32[]{:T(128)} %bitcast.17, s32[512]{0:T(512)S(1)} %get-tuple-element.63, f32[]{:T(128)} %bitcast.15, s32[512]{0:T(512)S(1)} %get-tuple-element.64, f32[]{:T(128)} %bitcast.13, s32[512]{0:T(512)S(1)} %get-tuple-element.65, f32[]{:T(128)} %bitcast.11, s32[512]{0:T(512)S(1)} %get-tuple-element.66, ...), kind=kOutput, calls=%fused_computation.30 | convolution fusion | flops 1651200000 | bytes 1337380 | tf_op jit(solution)/shard_map/dot_general | solution.py:51
  391.9 5.6 collective-permute-start.15
  398.8 14.5 %fusion.17 = f32[2048,128]{1,0:T(8,128)S(1)} fusion(f32[]{:T(128)} %bitcast.17, f32[]{:T(128)} %bitcast.15, f32[]{:T(128)} %bitcast.13, f32[]{:T(128)} %bitcast.11, f32[]{:T(128)} %bitcast.9, f32[]{:T(128)} %bitcast.7, f32[]{:T(128)} %bitcast.5, f32[]{:T(128)} %bitcast.3, f32[]{:T(128)} %bitcast.1, s32[516]{0:T(1024)S(1)} %iota_multiply_fusion, ...), kind=kOutput, calls=%fused_computation.38 | convolution fusion | flops 1650803712 | bytes 1388596 | tf_op jit(solution)/shard_map/dot_general | solution.py:51
  416.9 39.1 %psum.91 = f32[]{:T(128)} all-reduce(f32[]{:T(128)} %get-tuple-element.57), channel_id=1, replica_groups=mesh['row'=16,'col'=8] {'row'}, use_global_device_ids=true, to_apply=%region_11.12 | all-reduce | flops 1 | bytes 8 | tf_op jit(solution)/shard_map/psum | solution.py:90
  460.4 34.2 %psum.92 = f32[]{:T(128)} all-reduce(f32[]{:T(128)} %get-tuple-element.12), channel_id=1, replica_groups=mesh['row'=16,'col'=8] {'row'}, use_global_device_ids=true, to_apply=%region_13.14 | all-reduce | flops 1 | bytes 8 | tf_op jit(solution)/shard_map/psum | solution.py:90
  504.1 14.1 %fusion.10 = f32[512,128]{1,0:T(8,128)S(1)} fusion(f32[]{:T(128)} %bitcast.17, s32[512]{0:T(512)S(1)} %get-tuple-element.63, f32[]{:T(128)} %bitcast.15, s32[512]{0:T(512)S(1)} %get-tuple-element.64, f32[]{:T(128)} %bitcast.13, s32[512]{0:T(512)S(1)} %get-tuple-element.65, f32[]{:T(128)} %bitcast.11, s32[512]{0:T(512)S(1)} %get-tuple-element.66, ...), kind=kOutput, calls=%fused_computation.29 | convolution fusion | flops 1651200000 | bytes 1337380 | tf_op jit(solution)/shard_map/dot_general | solution.py:51
  518.3 5.6 collective-permute-start.19
  525.2 14.5 %fusion.16 = f32[2048,128]{1,0:T(8,128)S(1)} fusion(f32[]{:T(128)} %bitcast.17, f32[]{:T(128)} %bitcast.15, f32[]{:T(128)} %bitcast.13, f32[]{:T(128)} %bitcast.11, f32[]{:T(128)} %bitcast.9, f32[]{:T(128)} %bitcast.7, f32[]{:T(128)} %bitcast.5, f32[]{:T(128)} %bitcast.3, f32[]{:T(128)} %bitcast.1, s32[516]{0:T(1024)S(1)} %iota_multiply_fusion, ...), kind=kOutput, calls=%fused_computation.37 | convolution fusion | flops 1650803712 | bytes 1388596 | tf_op jit(solution)/shard_map/dot_general | solution.py:51
  543.3 39.1 %psum.93 = f32[]{:T(128)} all-reduce(f32[]{:T(128)} %get-tuple-element.59), channel_id=1, replica_groups=mesh['row'=16,'col'=8] {'row'}, use_global_device_ids=true, to_apply=%region_15.16 | all-reduce | flops 1 | bytes 8 | tf_op jit(solution)/shard_map/psum | solution.py:90
  587.0 33.8 %psum.94 = f32[]{:T(128)} all-reduce(f32[]{:T(128)} %get-tuple-element.10), channel_id=1, replica_groups=mesh['row'=16,'col'=8] {'row'}, use_global_device_ids=true, to_apply=%region_17.18 | all-reduce | flops 1 | bytes 8 | tf_op jit(solution)/shard_map/psum | solution.py:90
  630.5 14.1 %fusion.9 = f32[512,128]{1,0:T(8,128)S(1)} fusion(f32[]{:T(128)} %bitcast.17, s32[512]{0:T(512)S(1)} %get-tuple-element.63, f32[]{:T(128)} %bitcast.15, s32[512]{0:T(512)S(1)} %get-tuple-element.64, f32[]{:T(128)} %bitcast.13, s32[512]{0:T(512)S(1)} %get-tuple-element.65, f32[]{:T(128)} %bitcast.11, s32[512]{0:T(512)S(1)} %get-tuple-element.66, ...), kind=kOutput, calls=%fused_computation.28 | convolution fusion | flops 1651200000 | bytes 1337380 | tf_op jit(solution)/shard_map/dot_general | solution.py:51
  644.7 5.6 collective-permute-start.23
  651.7 15.5 %fusion.15 = f32[2048,128]{1,0:T(8,128)S(1)} fusion(f32[]{:T(128)} %bitcast.17, f32[]{:T(128)} %bitcast.15, f32[]{:T(128)} %bitcast.13, f32[]{:T(128)} %bitcast.11, f32[]{:T(128)} %bitcast.9, f32[]{:T(128)} %bitcast.7, f32[]{:T(128)} %bitcast.5, f32[]{:T(128)} %bitcast.3, f32[]{:T(128)} %bitcast.1, s32[516]{0:T(1024)S(1)} %iota_multiply_fusion, ...), kind=kOutput, calls=%fused_computation.36 | convolution fusion | flops 1650803712 | bytes 1388596 | tf_op jit(solution)/shard_map/dot_general | solution.py:51
  670.7 39.1 %psum.95 = f32[]{:T(128)} all-reduce(f32[]{:T(128)} %get-tuple-element.61), channel_id=1, replica_groups=mesh['row'=16,'col'=8] {'row'}, use_global_device_ids=true, to_apply=%region_19.20 | all-reduce | flops 1 | bytes 8 | tf_op jit(solution)/shard_map/psum | solution.py:90
  (117 shorter events, 86.9 us)
Async XLA Ops:
  7.2 39.3 %copy-start = (f32[2,96]{1,0:T(2,128)S(1)}, f32[2,96]{1,0:T(2,128)}, u32[]{:S(2)}) copy-start(f32[2,96]{1,0:T(2,128)} %param.13) | copy-start | bytes 2308
  7.2 134.7 %all-reduce.4.cloned.1.call-start = ((), (), s32[]{:S(2)}) async-start(), calls=%async_computation.1 | async-start | bytes 2883584 | tf_op jit(solution)/shard_map/psum | solution.py:75
  33.2 19.3 %collective-permute-start = (bf16[8,128]{0,1:T(8,128)(2,1)S(1)}, bf16[8,128]{0,1:T(8,128)(2,1)S(1)}, u32[]{:S(2)}, u32[]{:S(2)}) collective-permute-start(bf16[8,128]{0,1:T(8,128)(2,1)S(1)} %get-tuple-element.36), channel_id=1, source_target_pairs={{0,1},{1,2},{2,3},{3,4},{4,5},{5,6},{6,7},{7,0},{8,9},{9,10},{10,1... | collective-permute-start | bytes 6152 | tf_op jit(solution)/shard_map/ppermute | solution.py:20
  34.7 17.8 %collective-permute-start.1 = (bf16[8,128]{0,1:T(8,128)(2,1)S(1)}, bf16[8,128]{0,1:T(8,128)(2,1)S(1)}, u32[]{:S(2)}, u32[]{:S(2)}) collective-permute-start(bf16[8,128]{0,1:T(8,128)(2,1)S(1)} %get-tuple-element.37), channel_id=1, source_target_pairs={{1,0},{2,1},{3,2},{4,3},{5,4},{6,5},{7,6},{0,7},{9,8},{10,9},{11,1... | collective-permute-start | bytes 6152 | tf_op jit(solution)/shard_map/ppermute | solution.py:22
  47.4 12.4 %copy-start.4 = (f32[96,128]{1,0:T(8,128)S(1)}, f32[96,128]{1,0:T(8,128)}, u32[]{:S(2)}) copy-start(f32[96,128]{1,0:T(8,128)} %param.12) | copy-start | bytes 147460
  68.1 114.0 %all-gather.2.cloned.1.call-start = ((), (), s32[]{:S(2)}) async-start(), calls=%async_computation | async-start | bytes 1179648 | tf_op jit(solution)/shard_map/all_gather | solution.py:81
  182.8 6.6 collective-permute-start.4
  182.8 6.9 collective-permute-start.5
  189.7 20.8 %copy-start.6 = (f32[128,128]{1,0:T(8,128)S(1)}, f32[128,128]{1,0:T(8,128)}, u32[]{:S(2)}) copy-start(f32[128,128]{1,0:T(8,128)} %get-tuple-element.7) | copy-start | bytes 196612
  205.0 11.6 %collective-permute-start.6 = (f32[2,128]{1,0:T(2,128)S(1)}, f32[2,128]{1,0:T(2,128)S(1)}, u32[]{:S(2)}, u32[]{:S(2)}) collective-permute-start(f32[2,128]{1,0:T(2,128)S(1)} %get-tuple-element.34), channel_id=1, source_target_pairs={{0,8},{8,16},{16,24},{24,32},{32,40},{40,48},{48,56},{56,64},{64,7... | collective-permute-start | bytes 3080 | tf_op jit(solution)/shard_map/ppermute | solution.py:20
  205.1 11.5 %collective-permute-start.7 = (f32[2,128]{1,0:T(2,128)S(1)}, f32[2,128]{1,0:T(2,128)S(1)}, u32[]{:S(2)}, u32[]{:S(2)}) collective-permute-start(f32[2,128]{1,0:T(2,128)S(1)} %get-tuple-element.35), channel_id=1, source_target_pairs={{8,0},{16,8},{24,16},{32,24},{40,32},{48,40},{56,48},{64,56},{72,6... | collective-permute-start | bytes 3080 | tf_op jit(solution)/shard_map/ppermute | solution.py:22
  210.8 22.5 %collective-permute-start.2 = (f32[2,128]{0,1:T(8,128)S(1)}, f32[2,128]{0,1:T(8,128)S(1)}, u32[]{:S(2)}, u32[]{:S(2)}) collective-permute-start(f32[2,128]{0,1:T(8,128)S(1)} %get-tuple-element.32), channel_id=1, source_target_pairs={{0,8},{8,16},{16,24},{24,32},{32,40},{40,48},{48,56},{56,64},{64,7... | collective-permute-start | bytes 3080 | tf_op jit(solution)/shard_map/ppermute | solution.py:20
  210.9 22.5 %collective-permute-start.3 = (f32[2,128]{0,1:T(8,128)S(1)}, f32[2,128]{0,1:T(8,128)S(1)}, u32[]{:S(2)}, u32[]{:S(2)}) collective-permute-start(f32[2,128]{0,1:T(8,128)S(1)} %get-tuple-element.33), channel_id=1, source_target_pairs={{8,0},{16,8},{24,16},{32,24},{40,32},{48,40},{56,48},{64,56},{72,6... | collective-permute-start | bytes 3080 | tf_op jit(solution)/shard_map/ppermute | solution.py:22
  216.6 15.6 %copy-start.3 = (f32[2048,128]{1,0:T(8,128)S(1)}, f32[2048,128]{1,0:T(8,128)}, u32[]{:S(2)}) copy-start(f32[2048,128]{1,0:T(8,128)} %all-gather.2.cloned.1.call-done) | copy-start | bytes 3145732
  248.4 6.7 collective-permute-start.8
  248.4 6.9 collective-permute-start.9
  269.5 6.7 collective-permute-start.10
  269.6 7.1 collective-permute-start.11
  370.9 6.7 collective-permute-start.12
  371.0 6.7 collective-permute-start.13
  391.8 6.7 collective-permute-start.14
  391.9 6.9 collective-permute-start.15
  497.3 6.7 collective-permute-start.16
  497.4 6.7 collective-permute-start.17
  518.2 6.7 collective-permute-start.18
  518.3 6.9 collective-permute-start.19
  623.5 21.1 %copy-start.1 = (f32[2048,128]{1,0:T(8,128)}, f32[2048,128]{1,0:T(8,128)S(1)}, u32[]{:S(2)}) copy-start(f32[2048,128]{1,0:T(8,128)S(1)} %multiply_add_fusion) | copy-start | bytes 3145732
  623.5 6.9 collective-permute-start.20
  623.8 6.7 collective-permute-start.21
  644.7 6.7 collective-permute-start.22
  644.7 6.9 collective-permute-start.23
  650.4 17.8 %copy-start.2 = (f32[2048,128]{1,0:T(8,128)S(1)}, f32[2048,128]{1,0:T(8,128)}, u32[]{:S(2)}) copy-start(f32[2048,128]{1,0:T(8,128)} %copy-done.1) | copy-start | bytes 3145732
  (3 other events, 10.0 us)
Sparse Core Ops, SparseCore 0:
  68.2 73.6 all-reduce.3
  143.5 38.5 all-gather.1
where the time goes:
time: 728 us; the launch traced here: 722 us
  blocking collectives  284 us (39%)
  matrix products  199 us (27%)
  waiting for transfers between devices  113 us (16%)
  starting transfers between devices  66 us (9%)
  other arithmetic  30.2 us (4%)
  between operations  24.4 us (3%)
    psum x7, blocking collectives, inner_sum(): return lax.psum(jnp.sum(first_field * second_field), 'row')  258 us
    dot_general x12, matrix products, apply_band(): return jnp.dot(matrix, values.astype(jnp.float32), precision=FULL_PRECISION)  167 us
    ppermute x12, starting transfers between devices, extended(): lax.ppermute(head, axis, [((i + 1) % count, i) for i in range(count)])  63.5 us
    psum x1, waiting for transfers between devices, body(): column_gram, coarse_gram = lax.psum((column_part, coarse_part), 'col')  62 us
    all_gather x1, waiting for transfers between devices, body(): start_rows = lax.all_gather(row_start, 'col', axis=0, tiled=True)  39.1 us
    all_gather x1, blocking collectives, body(): columns = lax.all_gather(col_factor, 'row', axis=1, tiled=True)  25.9 us
  transfers between devices with their start and end apart: 26, of which 17 were waited for; matrix products, arithmetic and copies ran while one was open for 6% of the time, Pallas kernels for 0%

commit v1 on v0

--- a/solution.py
+++ b/solution.py
@@ -78,7 +78,8 @@
     hyper_gram = coarse_gram * band_gram
     multi_gram = column_gram * merged_gram
     multi_sums, hyper_sums = lax.psum((multi_part, hyper_part), "col")
-    start_rows = lax.all_gather(row_start, "col", axis=0, tiled=True)
+    outgoing = jnp.stack([row_start] * lax.axis_size("col"))
+    start_rows = jnp.concatenate(lax.all_to_all(outgoing, "col", 0, 0), axis=0)
 
     def fine_rim(values, breadth):
         return extended(values, (("row", 0),), breadth)

time: 728 us -> 672 us (0.923)
  waiting for transfers between devices: 113 us -> 52.4 us
    all_gather x1 -> x0, waiting for transfers between devices: 39.1 us -> none  [body(): start_rows = lax.all_gather(row_start, 'col', axis=0, tiled=True)]
    psum x1, waiting for transfers between devices: 62 us -> 40.2 us  [body(): column_gram, coarse_gram = lax.psum((column_part, coarse_part), 'col')]
  transfers between devices with their start and end apart: 26 -> 26, of which waited for: 17 -> 18; matrix products, arithmetic and copies ran while one was open for 6% -> 11% of each run, Pallas kernels for 0% -> 0%
where the time goes in v1:
time: 672 us; the launch traced here: 666 us
  blocking collectives  284 us (42%)
  matrix products  199 us (30%)
  starting transfers between devices  69.8 us (10%)
  waiting for transfers between devices  52.4 us (8%)
  other arithmetic  30.2 us (4%)
  between operations  24.4 us (4%)
    psum x7, blocking collectives, inner_sum(): return lax.psum(jnp.sum(first_field * second_field), 'row')  258 us
    dot_general x12, matrix products, apply_band(): return jnp.dot(matrix, values.astype(jnp.float32), precision=FULL_PRECISION)  166 us
    ppermute x12, starting transfers between devices, extended(): lax.ppermute(head, axis, [((i + 1) % count, i) for i in range(count)])  63.6 us
    psum x1, waiting for transfers between devices, body(): column_gram, coarse_gram = lax.psum((column_part, coarse_part), 'col')  40.2 us
    all_gather x1, blocking collectives, body(): columns = lax.all_gather(col_factor, 'row', axis=1, tiled=True)  25.9 us
  transfers between devices with their start and end apart: 26, of which 18 were waited for; matrix products, arithmetic and copies ran while one was open for 11% of the time, Pallas kernels for 0%

profile of v1, /device:TPU:0, one launch (start us, length us, event | category | flops | bytes accessed | tf_op | source)
XLA Modules:
  0.0 666.0 jit_solution(5651289299841598301)
XLA Ops:
  7.2 25.9 %all_gather.3 = bf16[512,128]{0,1:T(8,128)(2,1)S(1)} all-gather(bf16[512,8]{0,1:T(8,128)(2,1)} %param.11), channel_id=1, replica_groups=mesh['row'=16,'col'=8] {'row'}, dimensions={1}, use_global_device_ids=true | all-gather | bytes 139264 | tf_op jit(solution)/shard_map/all_gather | solution.py:58
  68.4 6.4 fusion.50
  74.9 8.2 %fusion.14 = f32[512,128]{0,1:T(8,128)} fusion(bf16[96,512,128]{2,1,0:T(8,128)(2,1)} %param.9, f32[128,128]{0,1:T(8,128)S(1)} %copy.10, f32[96,128]{1,0:T(8,128)S(1)} %copy-done.4), kind=kOutput, calls=%fused_computation.33 | convolution fusion | flops 1613758464 | bytes 12959744 | tf_op jit(solution)/shard_map/kij,kjr->ir/dot_general | solution.py:70
  83.1 5.5 collective-permute-start.5
  90.0 14.2 %fusion.13 = f32[512,128]{1,0:T(8,128)S(1)} fusion(f32[]{:T(128)} %bitcast.18, s32[512]{0:T(512)S(1)} %get-tuple-element.63, f32[]{:T(128)} %bitcast.16, s32[512]{0:T(512)S(1)} %get-tuple-element.64, f32[]{:T(128)} %bitcast.14, s32[512]{0:T(512)S(1)} %get-tuple-element.65, f32[]{:T(128)} %bitcast.12, s32[512]{0:T(512)S(1)} %get-tuple-element.66, ...), kind=kOutput, calls=%fused_computation.32 | convolution fusion | flops 1651200000 | bytes 1337380 | tf_op jit(solution)/shard_map/dot_general | solution.py:51
  104.3 5.8 collective-permute-start.7
  111.4 14.8 %fusion.19 = f32[2048,128]{1,0:T(8,128)S(1)} fusion(f32[]{:T(128)} %bitcast.18, f32[]{:T(128)} %bitcast.16, f32[]{:T(128)} %bitcast.14, f32[]{:T(128)} %bitcast.12, f32[]{:T(128)} %bitcast.10, f32[]{:T(128)} %bitcast.8, f32[]{:T(128)} %bitcast.6, f32[]{:T(128)} %bitcast.4, f32[]{:T(128)} %bitcast.2, s32[516]{0:T(1024)S(1)} %iota_multiply_fusion, ...), kind=kOutput, calls=%fused_computation.40 | convolution fusion | flops 1650803712 | bytes 1388596 | tf_op jit(solution)/shard_map/dot_general | solution.py:51
  126.2 40.2 %all-reduce.4.cloned.1.call-done = (f32[128,128]{1,0:T(8,128)}, f32[128,128]{1,0:T(8,128)}, f32[2048,128]{1,0:T(8,128)}, f32[512,128]{0,1:T(8,128)}) async-done(((f32[128,128]{1,0:T(8,128)}, f32[128,128]{1,0:T(8,128)}, f32[2048,128]{1,0:T(8,128)}, f32[512,128]{0,1:T(8,128)}), (f32[128,128]{1,0:T(8,128)}, f32[128,128]{1,0:T(8,128)}, f32[2048,128]{1,0:T(8,128)}, ...) | async-done | bytes 1441808 | tf_op jit(solution)/shard_map/psum | solution.py:75
  169.8 5.5 collective-permute-start.3
  177.4 14.9 %fusion.3 = f32[2048,128]{1,0:T(8,128)S(1)} fusion(f32[2048,128]{1,0:T(8,128)S(1)} %fusion.5, f32[2048,128]{1,0:T(8,128)S(1)} %copy-done.7, f32[]{:T(128)} %bitcast.18, f32[]{:T(128)} %bitcast.16, f32[]{:T(128)} %bitcast.14, f32[]{:T(128)} %bitcast.12, f32[]{:T(128)} %bitcast.10, f32[]{:T(128)} %bitcast.8, f32[]{:T(128)} %bitcast.6, f32[]{:T(128)} %bitcast.4, ...), kind=kOutput, calls=%fused_computation.18 | convolution fusion | flops 1651328000 | bytes 3485748 | tf_op jit(solution)/shard_map/dot_general | solution.py:51
  192.4 5.5 collective-permute-start.9
  199.3 14.2 %fusion.12 = f32[512,128]{1,0:T(8,128)S(1)} fusion(f32[]{:T(128)} %bitcast.18, s32[512]{0:T(512)S(1)} %get-tuple-element.63, f32[]{:T(128)} %bitcast.16, s32[512]{0:T(512)S(1)} %get-tuple-element.64, f32[]{:T(128)} %bitcast.14, s32[512]{0:T(512)S(1)} %get-tuple-element.65, f32[]{:T(128)} %bitcast.12, s32[512]{0:T(512)S(1)} %get-tuple-element.66, ...), kind=kOutput, calls=%fused_computation.31 | convolution fusion | flops 1651200000 | bytes 1337380 | tf_op jit(solution)/shard_map/dot_general | solution.py:51
  213.6 5.8 collective-permute-start.11
  220.7 14.6 %fusion.18 = f32[2048,128]{1,0:T(8,128)S(1)} fusion(f32[]{:T(128)} %bitcast.18, f32[]{:T(128)} %bitcast.16, f32[]{:T(128)} %bitcast.14, f32[]{:T(128)} %bitcast.12, f32[]{:T(128)} %bitcast.10, f32[]{:T(128)} %bitcast.8, f32[]{:T(128)} %bitcast.6, f32[]{:T(128)} %bitcast.4, f32[]{:T(128)} %bitcast.2, s32[516]{0:T(1024)S(1)} %iota_multiply_fusion, ...), kind=kOutput, calls=%fused_computation.39 | convolution fusion | flops 1650803712 | bytes 1388596 | tf_op jit(solution)/shard_map/dot_general | solution.py:51
  238.0 39.1 %all-reduce = (f32[]{:T(128)}, f32[]{:T(128)}) all-reduce(f32[]{:T(128)} %get-tuple-element.3, f32[]{:T(128)} %get-tuple-element.2), channel_id=1, replica_groups=mesh['row'=16,'col'=8] {'row'}, use_global_device_ids=true, to_apply=%region_5.6 | all-reduce | flops 2 | bytes 16 | tf_op jit(solution)/shard_map/psum | solution.py:91
  279.3 33.9 %psum.90 = f32[]{:T(128)} all-reduce(f32[]{:T(128)} %multiply_reduce_fusion.5), channel_id=1, replica_groups=mesh['row'=16,'col'=8] {'row'}, use_global_device_ids=true, to_apply=%region_9.10 | all-reduce | flops 1 | bytes 8 | tf_op jit(solution)/shard_map/psum | solution.py:91
  314.8 5.3 collective-permute-start.13
  321.5 14.2 %fusion.11 = f32[512,128]{1,0:T(8,128)S(1)} fusion(f32[]{:T(128)} %bitcast.18, s32[512]{0:T(512)S(1)} %get-tuple-element.63, f32[]{:T(128)} %bitcast.16, s32[512]{0:T(512)S(1)} %get-tuple-element.64, f32[]{:T(128)} %bitcast.14, s32[512]{0:T(512)S(1)} %get-tuple-element.65, f32[]{:T(128)} %bitcast.12, s32[512]{0:T(512)S(1)} %get-tuple-element.66, ...), kind=kOutput, calls=%fused_computation.30 | convolution fusion | flops 1651200000 | bytes 1337380 | tf_op jit(solution)/shard_map/dot_general | solution.py:51
  335.8 5.6 collective-permute-start.15
  342.7 14.6 %fusion.17 = f32[2048,128]{1,0:T(8,128)S(1)} fusion(f32[]{:T(128)} %bitcast.18, f32[]{:T(128)} %bitcast.16, f32[]{:T(128)} %bitcast.14, f32[]{:T(128)} %bitcast.12, f32[]{:T(128)} %bitcast.10, f32[]{:T(128)} %bitcast.8, f32[]{:T(128)} %bitcast.6, f32[]{:T(128)} %bitcast.4, f32[]{:T(128)} %bitcast.2, s32[516]{0:T(1024)S(1)} %iota_multiply_fusion, ...), kind=kOutput, calls=%fused_computation.38 | convolution fusion | flops 1650803712 | bytes 1388596 | tf_op jit(solution)/shard_map/dot_general | solution.py:51
  360.9 39.1 %psum.91 = f32[]{:T(128)} all-reduce(f32[]{:T(128)} %get-tuple-element.57), channel_id=1, replica_groups=mesh['row'=16,'col'=8] {'row'}, use_global_device_ids=true, to_apply=%region_11.12 | all-reduce | flops 1 | bytes 8 | tf_op jit(solution)/shard_map/psum | solution.py:91
  404.4 34.2 %psum.92 = f32[]{:T(128)} all-reduce(f32[]{:T(128)} %get-tuple-element.12), channel_id=1, replica_groups=mesh['row'=16,'col'=8] {'row'}, use_global_device_ids=true, to_apply=%region_13.14 | all-reduce | flops 1 | bytes 8 | tf_op jit(solution)/shard_map/psum | solution.py:91
  441.4 5.3 collective-permute-start.17
  448.1 14.2 %fusion.10 = f32[512,128]{1,0:T(8,128)S(1)} fusion(f32[]{:T(128)} %bitcast.18, s32[512]{0:T(512)S(1)} %get-tuple-element.63, f32[]{:T(128)} %bitcast.16, s32[512]{0:T(512)S(1)} %get-tuple-element.64, f32[]{:T(128)} %bitcast.14, s32[512]{0:T(512)S(1)} %get-tuple-element.65, f32[]{:T(128)} %bitcast.12, s32[512]{0:T(512)S(1)} %get-tuple-element.66, ...), kind=kOutput, calls=%fused_computation.29 | convolution fusion | flops 1651200000 | bytes 1337380 | tf_op jit(solution)/shard_map/dot_general | solution.py:51
  462.4 5.6 collective-permute-start.19
  469.2 14.6 %fusion.16 = f32[2048,128]{1,0:T(8,128)S(1)} fusion(f32[]{:T(128)} %bitcast.18, f32[]{:T(128)} %bitcast.16, f32[]{:T(128)} %bitcast.14, f32[]{:T(128)} %bitcast.12, f32[]{:T(128)} %bitcast.10, f32[]{:T(128)} %bitcast.8, f32[]{:T(128)} %bitcast.6, f32[]{:T(128)} %bitcast.4, f32[]{:T(128)} %bitcast.2, s32[516]{0:T(1024)S(1)} %iota_multiply_fusion, ...), kind=kOutput, calls=%fused_computation.37 | convolution fusion | flops 1650803712 | bytes 1388596 | tf_op jit(solution)/shard_map/dot_general | solution.py:51
  487.4 39.1 %psum.93 = f32[]{:T(128)} all-reduce(f32[]{:T(128)} %get-tuple-element.59), channel_id=1, replica_groups=mesh['row'=16,'col'=8] {'row'}, use_global_device_ids=true, to_apply=%region_15.16 | all-reduce | flops 1 | bytes 8 | tf_op jit(solution)/shard_map/psum | solution.py:91
  531.2 33.8 %psum.94 = f32[]{:T(128)} all-reduce(f32[]{:T(128)} %get-tuple-element.10), channel_id=1, replica_groups=mesh['row'=16,'col'=8] {'row'}, use_global_device_ids=true, to_apply=%region_17.18 | all-reduce | flops 1 | bytes 8 | tf_op jit(solution)/shard_map/psum | solution.py:91
  574.7 14.2 %fusion.9 = f32[512,128]{1,0:T(8,128)S(1)} fusion(f32[]{:T(128)} %bitcast.18, s32[512]{0:T(512)S(1)} %get-tuple-element.63, f32[]{:T(128)} %bitcast.16, s32[512]{0:T(512)S(1)} %get-tuple-element.64, f32[]{:T(128)} %bitcast.14, s32[512]{0:T(512)S(1)} %get-tuple-element.65, f32[]{:T(128)} %bitcast.12, s32[512]{0:T(512)S(1)} %get-tuple-element.66, ...), kind=kOutput, calls=%fused_computation.28 | convolution fusion | flops 1651200000 | bytes 1337380 | tf_op jit(solution)/shard_map/dot_general | solution.py:51
  589.0 5.6 collective-permute-start.23
  595.9 15.5 %fusion.15 = f32[2048,128]{1,0:T(8,128)S(1)} fusion(f32[]{:T(128)} %bitcast.18, f32[]{:T(128)} %bitcast.16, f32[]{:T(128)} %bitcast.14, f32[]{:T(128)} %bitcast.12, f32[]{:T(128)} %bitcast.10, f32[]{:T(128)} %bitcast.8, f32[]{:T(128)} %bitcast.6, f32[]{:T(128)} %bitcast.4, f32[]{:T(128)} %bitcast.2, s32[516]{0:T(1024)S(1)} %iota_multiply_fusion, ...), kind=kOutput, calls=%fused_computation.36 | convolution fusion | flops 1650803712 | bytes 1388596 | tf_op jit(solution)/shard_map/dot_general | solution.py:51
  615.0 39.1 %psum.95 = f32[]{:T(128)} all-reduce(f32[]{:T(128)} %get-tuple-element.61), channel_id=1, replica_groups=mesh['row'=16,'col'=8] {'row'}, use_global_device_ids=true, to_apply=%region_19.20 | all-reduce | flops 1 | bytes 8 | tf_op jit(solution)/shard_map/psum | solution.py:91
  (115 shorter events, 87.3 us)
Async XLA Ops:
  7.2 55.9 %copy-start = (f32[2,96]{1,0:T(2,128)S(1)}, f32[2,96]{1,0:T(2,128)}, u32[]{:S(2)}) copy-start(f32[2,96]{1,0:T(2,128)} %param.13) | copy-start | bytes 2308
  7.2 55.9 %copy-start.4 = (f32[96,128]{1,0:T(8,128)S(1)}, f32[96,128]{1,0:T(8,128)}, u32[]{:S(2)}) copy-start(f32[96,128]{1,0:T(8,128)} %param.12) | copy-start | bytes 147460
  33.2 35.2 %collective-permute-start = (bf16[8,128]{0,1:T(8,128)(2,1)S(1)}, bf16[8,128]{0,1:T(8,128)(2,1)S(1)}, u32[]{:S(2)}, u32[]{:S(2)}) collective-permute-start(bf16[8,128]{0,1:T(8,128)(2,1)S(1)} %get-tuple-element.36), channel_id=1, source_target_pairs={{0,1},{1,2},{2,3},{3,4},{4,5},{5,6},{6,7},{7,0},{8,9},{9,10},{10,1... | collective-permute-start | bytes 6152 | tf_op jit(solution)/shard_map/ppermute | solution.py:20
  34.7 33.7 %collective-permute-start.1 = (bf16[8,128]{0,1:T(8,128)(2,1)S(1)}, bf16[8,128]{0,1:T(8,128)(2,1)S(1)}, u32[]{:S(2)}, u32[]{:S(2)}) collective-permute-start(bf16[8,128]{0,1:T(8,128)(2,1)S(1)} %get-tuple-element.37), channel_id=1, source_target_pairs={{1,0},{2,1},{3,2},{4,3},{5,4},{6,5},{7,6},{0,7},{9,8},{10,9},{11,1... | collective-permute-start | bytes 6152 | tf_op jit(solution)/shard_map/ppermute | solution.py:22
  39.3 43.7 %all-to-all-start = ((f32[8,256,128]{2,1,0:T(8,128)}), f32[8,256,128]{2,1,0:T(8,128)S(1)}, u32[]{:S(2)}, u32[]{:S(2)}) async-start(f32[8,256,128]{2,1,0:T(8,128)} %stack.2), calls=%async_computation | async-start | bytes 2097152 | tf_op jit(solution)/shard_map/all_to_all | solution.py:82
  42.9 123.6 %all-reduce.4.cloned.1.call-start = ((), (), s32[]{:S(2)}) async-start(), calls=%async_computation.1 | async-start | bytes 2883584 | tf_op jit(solution)/shard_map/psum | solution.py:75
  83.0 93.3 %copy-start.1 = (f32[8,256,128]{2,1,0:T(8,128)}, f32[8,256,128]{2,1,0:T(8,128)S(1)}, u32[]{:S(2)}) copy-start(f32[8,256,128]{2,1,0:T(8,128)S(1)} %all-to-all-done) | copy-start | bytes 3145732
  83.0 6.7 %collective-permute-start.4 = (f32[8,128]{1,0:T(8,128)S(1)}, f32[8,128]{1,0:T(8,128)S(1)}, u32[]{:S(2)}, u32[]{:S(2)}) collective-permute-start(f32[8,128]{1,0:T(8,128)S(1)} %get-tuple-element.22), channel_id=1, source_target_pairs={{0,8},{8,16},{16,24},{24,32},{32,40},{40,48},{48,56},{56,64},{64,7... | collective-permute-start | bytes 12296 | tf_op jit(solution)/shard_map/ppermute | solution.py:20
  83.1 6.9 %collective-permute-start.5 = (f32[8,128]{1,0:T(8,128)S(1)}, f32[8,128]{1,0:T(8,128)S(1)}, u32[]{:S(2)}, u32[]{:S(2)}) collective-permute-start(f32[8,128]{1,0:T(8,128)S(1)} %get-tuple-element.23), channel_id=1, source_target_pairs={{8,0},{16,8},{24,16},{32,24},{40,32},{48,40},{56,48},{64,56},{72,6... | collective-permute-start | bytes 12296 | tf_op jit(solution)/shard_map/ppermute | solution.py:22
  104.2 6.7 %collective-permute-start.6 = (f32[2,128]{1,0:T(2,128)S(1)}, f32[2,128]{1,0:T(2,128)S(1)}, u32[]{:S(2)}, u32[]{:S(2)}) collective-permute-start(f32[2,128]{1,0:T(2,128)S(1)} %get-tuple-element.34), channel_id=1, source_target_pairs={{0,8},{8,16},{16,24},{24,32},{32,40},{40,48},{48,56},{56,64},{64,7... | collective-permute-start | bytes 3080 | tf_op jit(solution)/shard_map/ppermute | solution.py:20
  104.3 7.1 %collective-permute-start.7 = (f32[2,128]{1,0:T(2,128)S(1)}, f32[2,128]{1,0:T(2,128)S(1)}, u32[]{:S(2)}, u32[]{:S(2)}) collective-permute-start(f32[2,128]{1,0:T(2,128)S(1)} %get-tuple-element.35), channel_id=1, source_target_pairs={{8,0},{16,8},{24,16},{32,24},{40,32},{48,40},{56,48},{64,56},{72,6... | collective-permute-start | bytes 3080 | tf_op jit(solution)/shard_map/ppermute | solution.py:22
  166.4 11.0 %copy-start.7 = (f32[2048,128]{1,0:T(8,128)S(1)}, f32[2048,128]{1,0:T(8,128)}, u32[]{:S(2)}) copy-start(f32[2048,128]{1,0:T(8,128)} %get-tuple-element.8) | copy-start | bytes 3145732
  169.8 7.6 %collective-permute-start.2 = (f32[2,128]{0,1:T(8,128)S(1)}, f32[2,128]{0,1:T(8,128)S(1)}, u32[]{:S(2)}, u32[]{:S(2)}) collective-permute-start(f32[2,128]{0,1:T(8,128)S(1)} %get-tuple-element.32), channel_id=1, source_target_pairs={{0,8},{8,16},{16,24},{24,32},{32,40},{40,48},{48,56},{56,64},{64,7... | collective-permute-start | bytes 3080 | tf_op jit(solution)/shard_map/ppermute | solution.py:20
  169.8 7.6 %collective-permute-start.3 = (f32[2,128]{0,1:T(8,128)S(1)}, f32[2,128]{0,1:T(8,128)S(1)}, u32[]{:S(2)}, u32[]{:S(2)}) collective-permute-start(f32[2,128]{0,1:T(8,128)S(1)} %get-tuple-element.33), channel_id=1, source_target_pairs={{8,0},{16,8},{24,16},{32,24},{40,32},{48,40},{56,48},{64,56},{72,6... | collective-permute-start | bytes 3080 | tf_op jit(solution)/shard_map/ppermute | solution.py:22
  192.3 6.7 %collective-permute-start.8 = (f32[8,128]{1,0:T(8,128)S(1)}, f32[8,128]{1,0:T(8,128)S(1)}, u32[]{:S(2)}, u32[]{:S(2)}) collective-permute-start(f32[8,128]{1,0:T(8,128)S(1)} %get-tuple-element.20), channel_id=1, source_target_pairs={{0,8},{8,16},{16,24},{24,32},{32,40},{40,48},{48,56},{56,64},{64,7... | collective-permute-start | bytes 12296 | tf_op jit(solution)/shard_map/ppermute | solution.py:20
  192.4 6.9 %collective-permute-start.9 = (f32[8,128]{1,0:T(8,128)S(1)}, f32[8,128]{1,0:T(8,128)S(1)}, u32[]{:S(2)}, u32[]{:S(2)}) collective-permute-start(f32[8,128]{1,0:T(8,128)S(1)} %get-tuple-element.21), channel_id=1, source_target_pairs={{8,0},{16,8},{24,16},{32,24},{40,32},{48,40},{56,48},{64,56},{72,6... | collective-permute-start | bytes 12296 | tf_op jit(solution)/shard_map/ppermute | solution.py:22
  213.5 6.7 %collective-permute-start.10 = (f32[2,128]{1,0:T(2,128)S(1)}, f32[2,128]{1,0:T(2,128)S(1)}, u32[]{:S(2)}, u32[]{:S(2)}) collective-permute-start(f32[2,128]{1,0:T(2,128)S(1)} %get-tuple-element.30), channel_id=1, source_target_pairs={{0,8},{8,16},{16,24},{24,32},{32,40},{40,48},{48,56},{56,64},{64,7... | collective-permute-start | bytes 3080 | tf_op jit(solution)/shard_map/ppermute | solution.py:20
  213.6 7.1 %collective-permute-start.11 = (f32[2,128]{1,0:T(2,128)S(1)}, f32[2,128]{1,0:T(2,128)S(1)}, u32[]{:S(2)}, u32[]{:S(2)}) collective-permute-start(f32[2,128]{1,0:T(2,128)S(1)} %get-tuple-element.31), channel_id=1, source_target_pairs={{8,0},{16,8},{24,16},{32,24},{40,32},{48,40},{56,48},{64,56},{72,6... | collective-permute-start | bytes 3080 | tf_op jit(solution)/shard_map/ppermute | solution.py:22
  314.8 6.7 %collective-permute-start.12 = (f32[8,128]{1,0:T(8,128)S(1)}, f32[8,128]{1,0:T(8,128)S(1)}, u32[]{:S(2)}, u32[]{:S(2)}) collective-permute-start(f32[8,128]{1,0:T(8,128)S(1)} %get-tuple-element.18), channel_id=1, source_target_pairs={{0,8},{8,16},{16,24},{24,32},{32,40},{40,48},{48,56},{56,64},{64,7... | collective-permute-start | bytes 12296 | tf_op jit(solution)/shard_map/ppermute | solution.py:20
  314.8 6.7 %collective-permute-start.13 = (f32[8,128]{1,0:T(8,128)S(1)}, f32[8,128]{1,0:T(8,128)S(1)}, u32[]{:S(2)}, u32[]{:S(2)}) collective-permute-start(f32[8,128]{1,0:T(8,128)S(1)} %get-tuple-element.19), channel_id=1, source_target_pairs={{8,0},{16,8},{24,16},{32,24},{40,32},{48,40},{56,48},{64,56},{72,6... | collective-permute-start | bytes 12296 | tf_op jit(solution)/shard_map/ppermute | solution.py:22
  335.7 6.7 %collective-permute-start.14 = (f32[2,128]{1,0:T(2,128)S(1)}, f32[2,128]{1,0:T(2,128)S(1)}, u32[]{:S(2)}, u32[]{:S(2)}) collective-permute-start(f32[2,128]{1,0:T(2,128)S(1)} %get-tuple-element.28), channel_id=1, source_target_pairs={{0,8},{8,16},{16,24},{24,32},{32,40},{40,48},{48,56},{56,64},{64,7... | collective-permute-start | bytes 3080 | tf_op jit(solution)/shard_map/ppermute | solution.py:20
  335.8 6.9 %collective-permute-start.15 = (f32[2,128]{1,0:T(2,128)S(1)}, f32[2,128]{1,0:T(2,128)S(1)}, u32[]{:S(2)}, u32[]{:S(2)}) collective-permute-start(f32[2,128]{1,0:T(2,128)S(1)} %get-tuple-element.29), channel_id=1, source_target_pairs={{8,0},{16,8},{24,16},{32,24},{40,32},{48,40},{56,48},{64,56},{72,6... | collective-permute-start | bytes 3080 | tf_op jit(solution)/shard_map/ppermute | solution.py:22
  441.4 6.7 %collective-permute-start.16 = (f32[8,128]{1,0:T(8,128)S(1)}, f32[8,128]{1,0:T(8,128)S(1)}, u32[]{:S(2)}, u32[]{:S(2)}) collective-permute-start(f32[8,128]{1,0:T(8,128)S(1)} %get-tuple-element.16), channel_id=1, source_target_pairs={{0,8},{8,16},{16,24},{24,32},{32,40},{40,48},{48,56},{56,64},{64,7... | collective-permute-start | bytes 12296 | tf_op jit(solution)/shard_map/ppermute | solution.py:20
  441.4 6.7 %collective-permute-start.17 = (f32[8,128]{1,0:T(8,128)S(1)}, f32[8,128]{1,0:T(8,128)S(1)}, u32[]{:S(2)}, u32[]{:S(2)}) collective-permute-start(f32[8,128]{1,0:T(8,128)S(1)} %get-tuple-element.17), channel_id=1, source_target_pairs={{8,0},{16,8},{24,16},{32,24},{40,32},{48,40},{56,48},{64,56},{72,6... | collective-permute-start | bytes 12296 | tf_op jit(solution)/shard_map/ppermute | solution.py:22
  462.3 6.7 %collective-permute-start.18 = (f32[2,128]{1,0:T(2,128)S(1)}, f32[2,128]{1,0:T(2,128)S(1)}, u32[]{:S(2)}, u32[]{:S(2)}) collective-permute-start(f32[2,128]{1,0:T(2,128)S(1)} %get-tuple-element.26), channel_id=1, source_target_pairs={{0,8},{8,16},{16,24},{24,32},{32,40},{40,48},{48,56},{56,64},{64,7... | collective-permute-start | bytes 3080 | tf_op jit(solution)/shard_map/ppermute | solution.py:20
  462.4 6.9 %collective-permute-start.19 = (f32[2,128]{1,0:T(2,128)S(1)}, f32[2,128]{1,0:T(2,128)S(1)}, u32[]{:S(2)}, u32[]{:S(2)}) collective-permute-start(f32[2,128]{1,0:T(2,128)S(1)} %get-tuple-element.27), channel_id=1, source_target_pairs={{8,0},{16,8},{24,16},{32,24},{40,32},{48,40},{56,48},{64,56},{72,6... | collective-permute-start | bytes 3080 | tf_op jit(solution)/shard_map/ppermute | solution.py:22
  567.7 21.2 %copy-start.2 = (f32[2048,128]{1,0:T(8,128)}, f32[2048,128]{1,0:T(8,128)S(1)}, u32[]{:S(2)}) copy-start(f32[2048,128]{1,0:T(8,128)S(1)} %multiply_add_fusion) | copy-start | bytes 3145732
  567.7 6.9 %collective-permute-start.20 = (f32[8,128]{1,0:T(8,128)S(1)}, f32[8,128]{1,0:T(8,128)S(1)}, u32[]{:S(2)}, u32[]{:S(2)}) collective-permute-start(f32[8,128]{1,0:T(8,128)S(1)} %get-tuple-element.14), channel_id=1, source_target_pairs={{0,8},{8,16},{16,24},{24,32},{32,40},{40,48},{48,56},{56,64},{64,7... | collective-permute-start | bytes 12296 | tf_op jit(solution)/shard_map/ppermute | solution.py:20
  568.0 6.7 %collective-permute-start.21 = (f32[8,128]{1,0:T(8,128)S(1)}, f32[8,128]{1,0:T(8,128)S(1)}, u32[]{:S(2)}, u32[]{:S(2)}) collective-permute-start(f32[8,128]{1,0:T(8,128)S(1)} %get-tuple-element.15), channel_id=1, source_target_pairs={{8,0},{16,8},{24,16},{32,24},{40,32},{48,40},{56,48},{64,56},{72,6... | collective-permute-start | bytes 12296 | tf_op jit(solution)/shard_map/ppermute | solution.py:22
  588.9 6.7 %collective-permute-start.22 = (f32[2,128]{1,0:T(2,128)S(1)}, f32[2,128]{1,0:T(2,128)S(1)}, u32[]{:S(2)}, u32[]{:S(2)}) collective-permute-start(f32[2,128]{1,0:T(2,128)S(1)} %get-tuple-element.24), channel_id=1, source_target_pairs={{0,8},{8,16},{16,24},{24,32},{32,40},{40,48},{48,56},{56,64},{64,7... | collective-permute-start | bytes 3080 | tf_op jit(solution)/shard_map/ppermute | solution.py:20
  589.0 6.9 %collective-permute-start.23 = (f32[2,128]{1,0:T(2,128)S(1)}, f32[2,128]{1,0:T(2,128)S(1)}, u32[]{:S(2)}, u32[]{:S(2)}) collective-permute-start(f32[2,128]{1,0:T(2,128)S(1)} %get-tuple-element.25), channel_id=1, source_target_pairs={{8,0},{16,8},{24,16},{32,24},{40,32},{48,40},{56,48},{64,56},{72,6... | collective-permute-start | bytes 3080 | tf_op jit(solution)/shard_map/ppermute | solution.py:22
  594.6 17.8 %copy-start.3 = (f32[2048,128]{1,0:T(8,128)S(1)}, f32[2048,128]{1,0:T(8,128)}, u32[]{:S(2)}) copy-start(f32[2048,128]{1,0:T(8,128)} %copy-done.2) | copy-start | bytes 3145732
  (2 other events, 16.7 us)
Sparse Core Ops, SparseCore 0:
  89.7 76.6 all-reduce.3
